TPU v7x, 256 devices: a whole 4x4x8 slice. The times are simulated.
256 devices in a mesh: aux: 64 (over x, z, core), pair: 4 (over y).
Axes of the slice: x: 4, y: 4, z: 8, core: 2. Of those that a mesh axis runs over, the one named last changes fastest.
Arguments:
- shell_ints: bfloat16 [16384, 16, 64, 64], P('aux', 'pair'), may hold values from -0.119628906 to 0.119628906
- block_ids: int32 [16, 2], P('pair'), may hold values from 0 to 15
- block_count: int32 [4], P('pair'), may hold values from 1 to 4, 10 in all
- occ_coef: bfloat16 [16, 64, 512], replicated, may hold values from -0.75 to 0.75
- occ_pick: int32 [512], replicated, may hold values from 0 to 511, each once
- vir_coef: bfloat16 [16, 64, 384], replicated, may hold values from -0.1875 to 0.1875
- occ_energy: float32 [512], replicated, may hold values from -1.5 to -0.3
- vir_energy: float32 [384], replicated, may hold values from 0.2 to 3
Outputs:
- pair_energy: float32 [64], P('aux')
- vir_density: float32 [384, 384], P('pair')
Inputs may be any that keep to these rules, and one draw needn't show every extreme that they name: `block_ids`: basis block numbers of the mu and nu side. `block_count`: the busiest group holds exactly 4 live blocks. `occ_pick`: each of the 512 numbers appears once.
All inputs are finite; a program needn't handle non-finite values.
Results may differ from a plain program's by a relative error of at most 0.01.
Values may be sent and summed in bfloat16 or wider, within the bound.
A program may use at most 128 MiB of HBM per device.

v0:
```python
import jax
import jax.numpy as jnp
from jax import lax
from jax.sharding import PartitionSpec as P


def shifted(value, axis, steps):
    count = lax.axis_size(axis)
    pairs = [(source, (source + steps) % count) for source in range(count)]
    return lax.ppermute(value, axis, pairs)


def group_part(half, vir_rows, nrows):
    slots, width, virtual = vir_rows.shape
    orbitals = half.shape[1]
    flat = half.reshape(nrows, orbitals, slots * width)
    total = jnp.einsum(
        "qik,ka->qia",
        flat,
        vir_rows.reshape(slots * width, virtual),
        preferred_element_type=jnp.float32,
    )
    return lax.optimization_barrier(total.astype(jnp.bfloat16)).astype(jnp.float32)


def slot_tables(ids, live, occ_coef, vir_coef, picker):
    blocks = jnp.arange(occ_coef.shape[0], dtype=jnp.int32)
    nu_onehot = (ids[:, 1][:, None] == blocks[None, :]).astype(jnp.bfloat16)
    mu_onehot = (ids[:, 0][:, None] == blocks[None, :]).astype(jnp.bfloat16) * live[:, None]
    occ_rows = jnp.einsum(
        "kt,tno->kno", nu_onehot, occ_coef, preferred_element_type=jnp.float32
    ).astype(jnp.bfloat16)
    occ_sel = jnp.einsum(
        "kno,oi->kni", occ_rows, picker, preferred_element_type=jnp.float32
    ).astype(jnp.bfloat16)
    vir_rows = jnp.einsum(
        "kt,tma->kma", mu_onehot, vir_coef, preferred_element_type=jnp.float32
    ).astype(jnp.bfloat16)
    return (occ_sel, vir_rows)


def per_device(
    shell_ints, block_ids, block_count, occ_coef, occ_pick, vir_coef, occ_energy, vir_energy
):
    aux_rows, slots, width, _ = shell_ints.shape
    n_aux = lax.axis_size("aux")
    n_pair = lax.axis_size("pair")
    nocc = occ_coef.shape[2]
    virtual = vir_coef.shape[2]
    batch = occ_pick[:n_aux]
    levels = jnp.arange(nocc, dtype=jnp.int32)
    picker = (levels[:, None] == batch[None, :]).astype(jnp.bfloat16)
    live = (jnp.arange(slots, dtype=jnp.int32) < block_count[0]).astype(jnp.bfloat16)
    occ_sel, vir_rows = slot_tables(block_ids, live, occ_coef, vir_coef, picker)
    half = jnp.einsum(
        "qkmn,kni->qikm", shell_ints, occ_sel, preferred_element_type=jnp.float32
    ).astype(jnp.bfloat16)
    partial_value = group_part(half, vir_rows, aux_rows).astype(jnp.bfloat16)
    moved = lax.all_to_all(partial_value, "aux", split_axis=1, concat_axis=0, tiled=True)
    fitted = lax.psum_scatter(
        moved.astype(jnp.float32).astype(jnp.bfloat16), "pair", scatter_dimension=0, tiled=True
    )
    index = lax.axis_index("aux")
    own_rows = fitted[:, 0, :]
    mate_rows = shifted(own_rows, "aux", n_aux // 2)
    block = jnp.einsum("qa,qb->ab", own_rows, mate_rows, preferred_element_type=jnp.float32)
    coulomb = lax.psum(block.astype(jnp.bfloat16), "pair").astype(jnp.float32)
    mate = (index - n_aux // 2) % n_aux
    own_level = jnp.sum(jnp.where(levels == batch[index], occ_energy, 0.0))
    mate_level = jnp.sum(jnp.where(levels == batch[mate], occ_energy, 0.0))
    denom = own_level + mate_level - vir_energy[:, None] - vir_energy[None, :]
    amplitude = coulomb / denom
    energy = jnp.sum(amplitude * (2.0 * coulomb - coulomb.T)).reshape(1)
    share = virtual // n_pair
    first_row = lax.axis_index("pair") * share
    upper = lax.dynamic_slice_in_dim(amplitude, first_row, share, 0)
    column = lax.dynamic_slice_in_dim(amplitude, first_row, share, 1)
    left_rows = 2.0 * upper - column.T
    density_rows = jnp.dot(left_rows, amplitude.T, precision=lax.Precision.HIGHEST)
    vir_density = lax.psum(density_rows, "aux")
    return (energy, vir_density)


def solution(mesh):
    placed = (P("aux", "pair", None, None), P("pair", None), P("pair"), P(), P(), P(), P(), P())
    return jax.shard_map(
        per_device,
        mesh=mesh,
        in_specs=placed,
        out_specs=(P("aux"), P("pair", None)),
        check_vma=False,
    )
```

profile of v0, /device:TPU:1, one launch (start us, length us, event | category | flops | bytes accessed | tf_op | source)
XLA Modules:
  0.0 760.6 jit_solution(14656463893109439184)
XLA Ops:
  7.2 0.0 copy-start
  7.2 0.0 reduce-scatter.2.cloned.1.call-start
  7.2 0.8 slice_bitcast_fusion
  8.0 0.7 slice.10
  9.3 0.0 copy-done
  9.4 0.7 fusion.3
  10.1 9.2 %fusion.9 = bf16[4,64,256,64]{2,1,3,0:T(8,128)(2,1)} fusion(bf16[256,4,64,64]{0,3,2,1:T(8,128)(2,1)} %param.8, bf16[4,64,512]{2,0,1:T(4,128)(2,1)S(1)} %fusion.3, s32[64]{0:T(128)S(1)} %slice.10), kind=kOutput, calls=%fused_computation.14 | convolution fusion | flops 553697280 | bytes 17039616 | tf_op jit(solution)/shard_map/qkmn,kni->qikm/dot_general | solution.py:55
  19.3 0.0 copy-done.1
  19.3 0.5 fusion.5
  19.8 26.9 %bitcast_convert_fusion = bf16[256,64,384]{2,0,1:T(8,128)(2,1)} fusion(bf16[4,64,256,64]{2,1,3,0:T(8,128)(2,1)} %fusion.9, bf16[4,64,384]{2,0,1:T(4,128)(2,1)S(1)} %fusion.5), kind=kOutput, calls=%fused_computation | convolution fusion | flops 3227516928 | bytes 21168128 | tf_op jit(solution)/shard_map/qik,ka->qia/dot_general | solution.py:17
  46.7 289.0 %all_to_all.18 = bf16[256,64,384]{2,0,1:T(8,128)(2,1)} all-to-all(bf16[256,64,384]{2,0,1:T(8,128)(2,1)} %bitcast_convert_fusion), channel_id=1, replica_groups=mesh['aux'=64,'pair'=4] {'aux'}, dimensions={1} | all-to-all | bytes 25165824 | tf_op jit(solution)/shard_map/all_to_all | solution.py:59
  335.8 0.0 reduce-scatter.2.cloned.1.call-update
  335.8 0.0 all-reduce.3.cloned.1.call-start
  335.8 113.9 %reduce-scatter.2.cloned.1.call-done = bf16[4096,1,384]{2,0,1:T(8,128)(2,1)} async-done(((bf16[16384,1,384]{2,0,1:T(8,128)(2,1)}), bf16[4096,1,384]{2,0,1:T(8,128)(2,1)}) %reduce-scatter.2.cloned.1.call-update) | async-done | bytes 3145744 | tf_op jit(solution)/shard_map/reduce_scatter | solution.py:60
  449.7 2.7 collective-permute-start
  452.4 0.6 fusion.34
  453.0 67.5 %collective-permute-done = bf16[4096,384]{1,0:T(8,128)(2,1)} collective-permute-done((bf16[4096,384]{1,0:T(8,128)(2,1)}, bf16[4096,384]{1,0:T(8,128)(2,1)}, u32[]{:S(2)}, u32[]{:S(2)}) %collective-permute-start) | collective-permute-done | bytes 3145760 | tf_op jit(solution)/shard_map/ppermute | solution.py:10
  520.5 5.4 convolution_convert_fusion
  525.9 0.0 all-reduce.3.cloned.1.call-update
  525.9 0.0 all-reduce.5.cloned.1.call-start
  526.0 0.0 copy-done.3
  526.0 2.0 select_reduce_fusion
  529.4 0.0 copy-done.2
  529.4 42.2 %all-reduce.3.cloned.1.call-done = bf16[384,384]{1,0:T(8,128)(2,1)} async-done(((bf16[384,384]{1,0:T(8,128)(2,1)}), bf16[384,384]{1,0:T(8,128)(2,1)}) %all-reduce.3.cloned.1.call-update) | async-done | bytes 294928 | tf_op jit(solution)/shard_map/psum | solution.py:67
  571.5 1.1 copy.10
  572.7 1.9 subtract_divide_fusion
  574.5 0.1 constant_dynamic-slice_fusion
  574.6 0.1 copy.20
  574.8 1.2 fusion.15
  575.9 0.0 all-reduce.5.cloned.1.call-update
  576.0 176.5 %all-reduce.5.cloned.1.call-done = f32[96,384]{1,0:T(8,128)} async-done(((f32[96,384]{1,0:T(8,128)}), f32[96,384]{1,0:T(8,128)}) %all-reduce.5.cloned.1.call-update) | async-done | bytes 147472 | tf_op jit(solution)/shard_map/psum | solution.py:80
  752.5 1.6 copy.39
  (5 shorter events, 0.0 us)
Async XLA Ops:
  7.2 2.2 copy-start
  7.2 442.5 %reduce-scatter.2.cloned.1.call-start = ((), (), s32[]{:S(2)}) async-start(), calls=%async_computation.2 | async-start | bytes 15728640 | tf_op jit(solution)/shard_map/reduce_scatter | solution.py:60
  10.0 9.2 %copy-start.1 = (bf16[16,64,384]{2,1,0:T(8,128)(2,1)S(1)}, bf16[16,64,384]{2,1,0:T(8,128)(2,1)}, u32[]{:S(2)}) copy-start(bf16[16,64,384]{2,1,0:T(8,128)(2,1)} %param.13) | copy-start | bytes 2359300
  335.8 190.2 %copy-start.3 = (f32[512]{0:T(512)S(1)}, f32[512]{0:T(512)}, u32[]{:S(2)}) copy-start(f32[512]{0:T(512)} %param.14) | copy-start | bytes 6148
  335.8 193.6 %copy-start.2 = (f32[384]{0:T(512)S(1)}, f32[384]{0:T(512)}, u32[]{:S(2)}) copy-start(f32[384]{0:T(512)} %param.15) | copy-start | bytes 4612
  335.8 235.7 %all-reduce.3.cloned.1.call-start = ((), (), s32[]{:S(2)}) async-start(), calls=%async_computation.3 | async-start | bytes 589824 | tf_op jit(solution)/shard_map/psum | solution.py:67
  449.7 70.8 %collective-permute-start = (bf16[4096,384]{1,0:T(8,128)(2,1)}, bf16[4096,384]{1,0:T(8,128)(2,1)}, u32[]{:S(2)}, u32[]{:S(2)}) collective-permute-start(bf16[4096,384]{1,0:T(8,128)(2,1)} %bitcast.55), channel_id=1, source_target_pairs={{0,128},{4,132},{8,136},{12,140},{16,144},{20,148},{24,152},{28,15... | collective-permute-start | bytes 9437192 | tf_op jit(solution)/shard_map/ppermute | solution.py:10
  525.9 226.6 %all-reduce.5.cloned.1.call-start = ((), (), s32[]{:S(2)}) async-start(), calls=%async_computation.4 | async-start | bytes 294912 | tf_op jit(solution)/shard_map/psum | solution.py:80
Sparse Core Ops, SparseCore 0:
  335.9 113.7 reduce-scatter.1
  526.1 45.4 all-reduce.2
  576.1 176.3 all-reduce.4
where the time goes:
time: 761 us
  waiting for transfers between devices  400 us (53%)
  blocking collectives  289 us (38%)
  matrix products  43.9 us (6%)
  between operations  15.8 us (2%)
    all_to_all x1, blocking collectives, per_device(): lax.all_to_all(partial_value, 'aux', split_axis=1, concat_axis=0, tiled=T...  289 us
    psum x1, waiting for transfers between devices, per_device(): vir_density = lax.psum(density_rows, 'aux')  177 us
    reduce_scatter x1, waiting for transfers between devices, per_device(): lax.psum_scatter(moved.astype(jnp.float32).astype(jnp.bfloat16), 'pair',...  114 us
    ppermute x1, waiting for transfers between devices, shifted(): return lax.ppermute(value, axis, pairs)  67.5 us
    psum x1, waiting for transfers between devices, per_device(): coulomb = lax.psum(block.astype(jnp.bfloat16), 'pair').astype(jnp.float32)  42.2 us
    dot_general x1, matrix products, group_part(): jnp.einsum('qik,ka->qia', flat, vir_rows.reshape(slots * width, virtual),...  26.9 us
  transfers between devices with their start and end apart: 4, of which 4 were waited for; matrix products, arithmetic and copies ran while one was open for 0% of the time, Pallas kernels for 0%

commit v1 on v0

--- a/solution.py
+++ b/solution.py
@@ -77,7 +77,7 @@
     column = lax.dynamic_slice_in_dim(amplitude, first_row, share, 1)
     left_rows = 2.0 * upper - column.T
     density_rows = jnp.dot(left_rows, amplitude.T, precision=lax.Precision.HIGHEST)
-    vir_density = lax.psum(density_rows, "aux")
+    vir_density = jnp.sum(lax.all_gather(density_rows, "aux"), axis=0)
     return (energy, vir_density)
 
 

time: 761 us -> 676 us (0.89)
  waiting for transfers between devices: 400 us -> 312 us
    psum x1 -> x0, waiting for transfers between devices: 177 us -> none  [per_device(): vir_density = lax.psum(density_rows, 'aux')]
    all_gather x0 -> x1, waiting for transfers between devices: none -> 88.2 us  [per_device(): vir_density = jnp.sum(lax.all_gather(density_rows, 'aux'), axis=0)]
where the time goes in v1:
time: 676 us; the launch traced here: 675 us
  waiting for transfers between devices  312 us (46%)
  blocking collectives  289 us (43%)
  matrix products  43.9 us (6%)
  between operations  15.8 us (2%)
  other arithmetic  8.62 us (1%)
    all_to_all x1, blocking collectives, per_device(): lax.all_to_all(partial_value, 'aux', split_axis=1, concat_axis=0, tiled=T...  289 us
    reduce_scatter x1, waiting for transfers between devices, per_device(): lax.psum_scatter(moved.astype(jnp.float32).astype(jnp.bfloat16), 'pair',...  114 us
    all_gather x1, waiting for transfers between devices, per_device(): vir_density = jnp.sum(lax.all_gather(density_rows, 'aux'), axis=0)  88.2 us
    ppermute x1, waiting for transfers between devices, shifted(): return lax.ppermute(value, axis, pairs)  67.5 us
    psum x1, waiting for transfers between devices, per_device(): coulomb = lax.psum(block.astype(jnp.bfloat16), 'pair').astype(jnp.float32)  42.2 us
    dot_general x1, matrix products, group_part(): jnp.einsum('qik,ka->qia', flat, vir_rows.reshape(slots * width, virtual),...  26.9 us
  transfers between devices with their start and end apart: 4, of which 4 were waited for; matrix products, arithmetic and copies ran while one was open for 0% of the time, Pallas kernels for 0%

profile of v1, /device:TPU:1, one launch (start us, length us, event | category | flops | bytes accessed | tf_op | source)
XLA Modules:
  0.0 675.4 jit_solution(17699549484344440725)
XLA Ops:
  7.2 0.0 copy-start
  7.2 0.0 reduce-scatter.2.cloned.1.call-start
  7.2 0.8 slice_bitcast_fusion
  8.0 0.7 slice.10
  9.3 0.0 copy-done
  9.4 0.7 fusion.3
  10.1 9.2 %fusion.9 = bf16[4,64,256,64]{2,1,3,0:T(8,128)(2,1)} fusion(bf16[256,4,64,64]{0,3,2,1:T(8,128)(2,1)} %param.8, bf16[4,64,512]{2,0,1:T(4,128)(2,1)S(1)} %fusion.3, s32[64]{0:T(128)S(1)} %slice.10), kind=kOutput, calls=%fused_computation.14 | convolution fusion | flops 553697280 | bytes 17039616 | tf_op jit(solution)/shard_map/qkmn,kni->qikm/dot_general | solution.py:55
  19.3 0.0 copy-done.1
  19.3 0.5 fusion.5
  19.8 26.9 %bitcast_convert_fusion = bf16[256,64,384]{2,0,1:T(8,128)(2,1)} fusion(bf16[4,64,256,64]{2,1,3,0:T(8,128)(2,1)} %fusion.9, bf16[4,64,384]{2,0,1:T(4,128)(2,1)S(1)} %fusion.5), kind=kOutput, calls=%fused_computation | convolution fusion | flops 3227516928 | bytes 21168128 | tf_op jit(solution)/shard_map/qik,ka->qia/dot_general | solution.py:17
  46.7 289.0 %all_to_all.18 = bf16[256,64,384]{2,0,1:T(8,128)(2,1)} all-to-all(bf16[256,64,384]{2,0,1:T(8,128)(2,1)} %bitcast_convert_fusion), channel_id=1, replica_groups=mesh['aux'=64,'pair'=4] {'aux'}, dimensions={1} | all-to-all | bytes 25165824 | tf_op jit(solution)/shard_map/all_to_all | solution.py:59
  335.8 0.0 reduce-scatter.2.cloned.1.call-update
  335.8 0.0 all-reduce.2.cloned.1.call-start
  335.8 113.9 %reduce-scatter.2.cloned.1.call-done = bf16[4096,1,384]{2,0,1:T(8,128)(2,1)} async-done(((bf16[16384,1,384]{2,0,1:T(8,128)(2,1)}), bf16[4096,1,384]{2,0,1:T(8,128)(2,1)}) %reduce-scatter.2.cloned.1.call-update) | async-done | bytes 3145744 | tf_op jit(solution)/shard_map/reduce_scatter | solution.py:60
  449.7 2.7 collective-permute-start
  452.4 0.6 fusion.34
  453.0 67.5 %collective-permute-done = bf16[4096,384]{1,0:T(8,128)(2,1)} collective-permute-done((bf16[4096,384]{1,0:T(8,128)(2,1)}, bf16[4096,384]{1,0:T(8,128)(2,1)}, u32[]{:S(2)}, u32[]{:S(2)}) %collective-permute-start) | collective-permute-done | bytes 3145760 | tf_op jit(solution)/shard_map/ppermute | solution.py:10
  520.5 5.4 convolution_convert_fusion
  525.9 0.0 all-reduce.2.cloned.1.call-update
  525.9 0.0 all-gather.3.cloned.1.call-start
  526.0 0.0 copy-done.3
  526.0 2.0 select_reduce_fusion
  529.4 0.0 copy-done.2
  529.4 42.2 %all-reduce.2.cloned.1.call-done = bf16[384,384]{1,0:T(8,128)(2,1)} async-done(((bf16[384,384]{1,0:T(8,128)(2,1)}), bf16[384,384]{1,0:T(8,128)(2,1)}) %all-reduce.2.cloned.1.call-update) | async-done | bytes 294928 | tf_op jit(solution)/shard_map/psum | solution.py:67
  571.5 1.1 copy.10
  572.7 1.9 subtract_divide_fusion
  574.5 0.1 constant_dynamic-slice_fusion
  574.6 0.1 copy.20
  574.8 1.2 fusion.15
  575.9 0.0 all-gather.3.cloned.1.call-update
  576.0 88.2 %all-gather.3.cloned.1.call-done = f32[6144,384]{1,0:T(8,128)} async-done(((f32[96,384]{1,0:T(8,128)}), f32[6144,384]{1,0:T(8,128)}) %all-gather.3.cloned.1.call-update) | async-done | bytes 9437200 | tf_op jit(solution)/shard_map/all_gather | solution.py:80
  664.1 4.8 reduce_sum.39
  (5 shorter events, 0.0 us)
Async XLA Ops:
  7.2 2.2 copy-start
  7.2 442.5 %reduce-scatter.2.cloned.1.call-start = ((), (), s32[]{:S(2)}) async-start(), calls=%async_computation.2 | async-start | bytes 15728640 | tf_op jit(solution)/shard_map/reduce_scatter | solution.py:60
  10.0 9.2 %copy-start.1 = (bf16[16,64,384]{2,1,0:T(8,128)(2,1)S(1)}, bf16[16,64,384]{2,1,0:T(8,128)(2,1)}, u32[]{:S(2)}) copy-start(bf16[16,64,384]{2,1,0:T(8,128)(2,1)} %param.13) | copy-start | bytes 2359300
  335.8 190.2 %copy-start.3 = (f32[512]{0:T(512)S(1)}, f32[512]{0:T(512)}, u32[]{:S(2)}) copy-start(f32[512]{0:T(512)} %param.14) | copy-start | bytes 6148
  335.8 193.6 %copy-start.2 = (f32[384]{0:T(512)S(1)}, f32[384]{0:T(512)}, u32[]{:S(2)}) copy-start(f32[384]{0:T(512)} %param.15) | copy-start | bytes 4612
  335.8 235.7 %all-reduce.2.cloned.1.call-start = ((), (), s32[]{:S(2)}) async-start(), calls=%async_computation.3 | async-start | bytes 589824 | tf_op jit(solution)/shard_map/psum | solution.py:67
  449.7 70.8 %collective-permute-start = (bf16[4096,384]{1,0:T(8,128)(2,1)}, bf16[4096,384]{1,0:T(8,128)(2,1)}, u32[]{:S(2)}, u32[]{:S(2)}) collective-permute-start(bf16[4096,384]{1,0:T(8,128)(2,1)} %bitcast.57), channel_id=1, source_target_pairs={{0,128},{4,132},{8,136},{12,140},{16,144},{20,148},{24,152},{28,15... | collective-permute-start | bytes 9437192 | tf_op jit(solution)/shard_map/ppermute | solution.py:10
  525.9 138.2 %all-gather.3.cloned.1.call-start = ((), (), s32[]{:S(2)}) async-start(), calls=%async_computation.4 | async-start | bytes 9584640 | tf_op jit(solution)/shard_map/all_gather | solution.py:80
Sparse Core Ops, SparseCore 0:
  335.9 113.7 reduce-scatter.1
  526.1 45.4 all-reduce.1
  576.1 87.9 all-gather.2
